TPU v7x, 32 devices: a whole 2x2x4 slice. The times are simulated.
32 devices in a mesh: dp: 8 (over z, x), tensor: 4 (over y, core).
Axes of the slice: x: 2, y: 2, z: 4, core: 2. Of those that a mesh axis runs over, the one named last changes fastest.
Arguments:
- tokens: bfloat16 [16384, 1024], P('dp'), may hold values from -6 to 6
- segments: int32 [16, 1024], P('dp'), may hold values from 0 to 7, never falling along the last dimension, each value on 1 to 512 neighbouring positions
- w_qkv: bfloat16 [1024, 3, 1024], P(None, None, 'tensor'), may hold values from -0.1875 to 0.1875
- head_bias: float32 [2, 1024], P(None, 'tensor'), may hold values from -3 to 3
- w_out: bfloat16 [1024, 1024], P('tensor'), may hold values from -0.75 to 0.75
- w_in: bfloat16 [1024, 4096], P(None, 'tensor'), may hold values from -0.1875 to 0.1875
- unit_bias: float32 [4096], P('tensor'), may hold values from -3 to 3
- w_down: bfloat16 [4096, 1024], P('tensor'), may hold values from -0.09375 to 0.09375
- vectors: float32 [6, 1024], replicated, may hold values from 0.5 to 1.5
- cotangent: bfloat16 [16384, 1024], P('dp'), may hold values from -6 to 6
- err_qkv: float32 [8, 1024, 3, 1024], P('dp', None, None, 'tensor'), may hold values from -80 to 80
- err_out: float32 [8, 1024, 1024], P('dp', 'tensor'), may hold values from -80 to 80
- err_in: float32 [8, 1024, 4096], P('dp', None, 'tensor'), may hold values from -80 to 80
- err_down: float32 [8, 4096, 1024], P('dp', 'tensor'), may hold values from -80 to 80
- basis_qkv: float32 [8, 3, 1024], P(None, None, 'tensor'), may hold values from -6 to 6
- basis_out: float32 [32, 1024], P('tensor'), may hold values from -6 to 6
- basis_in: float32 [8, 4096], P(None, 'tensor'), may hold values from -6 to 6
- basis_down: float32 [32, 1024], P('tensor'), may hold values from -6 to 6
- mom_qkv: float32 [1024, 3, 1024], P(None, None, 'tensor'), may hold values from -5 to 5
- mom_head_bias: float32 [2, 1024], P(None, 'tensor'), may hold values from -10 to 10
- mom_out: float32 [1024, 1024], P('tensor'), may hold values from -5 to 5
- mom_in: float32 [1024, 4096], P(None, 'tensor'), may hold values from -5 to 5
- mom_unit_bias: float32 [4096], P('tensor'), may hold values from -10 to 10
- mom_down: float32 [4096, 1024], P('tensor'), may hold values from -5 to 5
- mom_vectors: float32 [6, 1024], replicated, may hold values from -28 to 28
Outputs:
- layer_out: bfloat16 [16384, 1024], P(('dp', 'tensor'))
- grad_tokens: float32 [16384, 1024], P(('dp', 'tensor'))
- grad_w_qkv: float32 [1024, 3, 1024], P(None, None, 'tensor')
- grad_head_bias: float32 [2, 1024], P(None, 'tensor')
- grad_w_out: float32 [1024, 1024], P('tensor')
- grad_w_in: float32 [1024, 4096], P(None, 'tensor')
- grad_unit_bias: float32 [4096], P('tensor')
- grad_w_down: float32 [4096, 1024], P('tensor')
- grad_vectors: float32 [6, 1024], replicated
- new_err_qkv: float32 [8, 1024, 3, 1024], P('dp', None, None, 'tensor')
- new_err_out: float32 [8, 1024, 1024], P('dp', 'tensor')
- new_err_in: float32 [8, 1024, 4096], P('dp', None, 'tensor')
- new_err_down: float32 [8, 4096, 1024], P('dp', 'tensor')
- new_basis_qkv: float32 [8, 3, 1024], P(None, None, 'tensor')
- new_basis_out: float32 [32, 1024], P('tensor')
- new_basis_in: float32 [8, 4096], P(None, 'tensor')
- new_basis_down: float32 [32, 1024], P('tensor')
- new_mom_qkv: float32 [1024, 3, 1024], P(None, None, 'tensor')
- new_mom_head_bias: float32 [2, 1024], P(None, 'tensor')
- new_mom_out: float32 [1024, 1024], P('tensor')
- new_mom_in: float32 [1024, 4096], P(None, 'tensor')
- new_mom_unit_bias: float32 [4096], P('tensor')
- new_mom_down: float32 [4096, 1024], P('tensor')
- new_mom_vectors: float32 [6, 1024], replicated
- new_w_qkv: float32 [1024, 3, 1024], P(None, None, 'tensor')
- new_head_bias: float32 [2, 1024], P(None, 'tensor')
- new_w_out: float32 [1024, 1024], P('tensor')
- new_w_in: float32 [1024, 4096], P(None, 'tensor')
- new_unit_bias: float32 [4096], P('tensor')
- new_w_down: float32 [4096, 1024], P('tensor')
- new_vectors: float32 [6, 1024], replicated
Inputs may be any that keep to these rules, and one draw needn't show every extreme that they name: `segments`: along a sequence the numbers never fall; each of its 8 documents holds 1 to 512 tokens, and one of them exactly 512.
All inputs are finite; a program needn't handle non-finite values.
Results may differ from a plain program's by a relative error of at most 0.02.
Values may be sent and summed in bfloat16 or wider, within the bound.
A program may use at most 256 MiB of HBM per device.

v0:
```python
from functools import partial
import math
import jax
import jax.numpy as jnp
from jax import lax
from jax.sharding import PartitionSpec as P

DH = 64
PRECISE = lax.Precision.HIGHEST
EPS_NORM = 1e-05
EPS_BASIS = 1e-08
MASKED = -1000000000.0


def norm_forward(values, gain, shift):
    row_mean = jnp.mean(values, axis=-1, keepdims=True)
    centred = values - row_mean
    variance = jnp.mean(centred * centred, axis=-1, keepdims=True)
    inverse = lax.rsqrt(variance + EPS_NORM)
    normed = centred * inverse
    return (normed * gain + shift, normed, inverse)


def norm_backward(grad_norm, normed, inverse, gain):
    scaled_grad = grad_norm * gain
    grad_mean = jnp.mean(scaled_grad, axis=-1, keepdims=True)
    along_norm = jnp.mean(scaled_grad * normed, axis=-1, keepdims=True)
    return inverse * (scaled_grad - grad_mean - normed * along_norm)


def times_trans(left_side, right_side):
    return lax.dot_general(
        left_side, right_side, (((1,), (1,)), ((), ())), preferred_element_type=jnp.float32
    )


def trans_times(left_side, right_side):
    return lax.dot_general(
        left_side, right_side, (((0,), (0,)), ((), ())), preferred_element_type=jnp.float32
    )


def left_of(matrix, factor):
    return lax.dot_general(
        matrix,
        factor,
        (((1,), (1,)), ((), ())),
        precision=PRECISE,
        preferred_element_type=jnp.float32,
    )


def right_of(basis, matrix):
    return lax.dot_general(
        basis,
        matrix,
        (((0,), (0,)), ((), ())),
        precision=PRECISE,
        preferred_element_type=jnp.float32,
    )


def orthonormal(factor):
    columns = []
    for position in range(factor.shape[-1]):
        column = factor[..., position]
        for earlier in columns:
            column = column - jnp.sum(earlier * column, axis=-1, keepdims=True) * earlier
        column = column / (jnp.sqrt(jnp.sum(column * column, axis=-1, keepdims=True)) + EPS_BASIS)
        columns.append(column)
    return jnp.stack(columns, axis=-1)


def masked_scores(queries, key_heads, seg_ids):
    scores = jnp.einsum("qhd,khd->hqk", queries, key_heads, preferred_element_type=jnp.float32)
    same_doc = seg_ids[:, None] == seg_ids[None, :]
    return jnp.where(same_doc[None], scores, MASKED)


def attend_forward(inputs_of):
    queries, key_heads, value_heads, seg_ids = inputs_of
    scores = masked_scores(queries, key_heads, seg_ids)
    highest = jnp.max(scores, axis=-1, keepdims=True)
    powers = jnp.exp(scores - highest)
    denominator = jnp.sum(powers, axis=-1, keepdims=True)
    weights = (powers / denominator).astype(jnp.bfloat16)
    mixed_heads = jnp.einsum(
        "hqk,khd->qhd", weights, value_heads, preferred_element_type=jnp.float32
    )
    return (mixed_heads.astype(jnp.bfloat16), highest[..., 0] + jnp.log(denominator[..., 0]))


def attend_backward(inputs_of):
    queries, key_heads, value_heads, seg_ids, grad_mixed, log_total = inputs_of
    scores = masked_scores(queries, key_heads, seg_ids)
    probability = jnp.exp(scores - log_total[..., None])
    grad_probs = jnp.einsum(
        "qhd,khd->hqk", grad_mixed, value_heads, preferred_element_type=jnp.float32
    )
    centre = jnp.sum(probability * grad_probs, axis=-1, keepdims=True)
    grad_scores = (probability * (grad_probs - centre)).astype(jnp.bfloat16)
    grad_query = jnp.einsum(
        "hqk,khd->qhd", grad_scores, key_heads, preferred_element_type=jnp.float32
    )
    grad_key = jnp.einsum("hqk,qhd->khd", grad_scores, queries, preferred_element_type=jnp.float32)
    grad_value = jnp.einsum(
        "hqk,qhd->khd",
        probability.astype(jnp.bfloat16),
        grad_mixed,
        preferred_element_type=jnp.float32,
    )
    return (
        grad_query.astype(jnp.bfloat16),
        grad_key.astype(jnp.bfloat16),
        grad_value.astype(jnp.bfloat16),
    )


def local(
    tokens,
    segments,
    w_qkv,
    head_bias,
    w_out,
    w_in,
    unit_bias,
    w_down,
    vectors,
    cotangent,
    err_qkv,
    err_out,
    err_in,
    err_down,
    basis_qkv,
    basis_out,
    basis_in,
    basis_down,
    mom_qkv,
    mom_head_bias,
    mom_out,
    mom_in,
    mom_unit_bias,
    mom_down,
    mom_vectors,
):
    token_count, model_width = tokens.shape
    seq_count, length = segments.shape
    head_slab = w_qkv.shape[2]
    head_count = head_slab // DH
    unit_slab = w_in.shape[1]
    rank_size = basis_in.shape[0]
    tensor_size = lax.axis_size("tensor")
    replicas = lax.axis_size("dp")
    share_rows = token_count // tensor_size
    tensor_place = lax.axis_index("tensor")
    row_start = tensor_place * share_rows
    head_scale = 1.0 / math.sqrt(DH)

    def own_rows(values):
        return lax.dynamic_slice_in_dim(values, row_start, share_rows, 0)

    flat_qkv = w_qkv.reshape(model_width, 3 * head_slab)
    projected = jnp.dot(tokens, flat_qkv, preferred_element_type=jnp.float32).reshape(
        token_count, 3, head_slab
    )
    head_shape = (seq_count, length, head_count, DH)
    queries = (
        ((projected[:, 0] + head_bias[0]) * head_scale).astype(jnp.bfloat16).reshape(head_shape)
    )
    key_heads = projected[:, 1].astype(jnp.bfloat16).reshape(head_shape)
    value_heads = (projected[:, 2] + head_bias[1]).astype(jnp.bfloat16).reshape(head_shape)
    mixed_heads, log_total = lax.map(attend_forward, (queries, key_heads, value_heads, segments))
    mixed_flat = mixed_heads.reshape(token_count, head_slab)
    attn_out = (
        lax.psum(jnp.dot(mixed_flat, w_out, preferred_element_type=jnp.float32), "tensor")
        + vectors[0]
    )
    first_norm, first_normed, first_inverse = norm_forward(
        tokens.astype(jnp.float32) + attn_out, vectors[2], vectors[3]
    )
    first_low = first_norm.astype(jnp.bfloat16)
    hidden = jnp.dot(first_low, w_in, preferred_element_type=jnp.float32) + unit_bias
    active, gelu_back = jax.vjp(partial(jax.nn.gelu, approximate=False), hidden)
    active_low = active.astype(jnp.bfloat16)
    grad_out_share = own_rows(cotangent).astype(jnp.float32)
    summed_input = (
        first_norm
        + lax.psum(jnp.dot(active_low, w_down, preferred_element_type=jnp.float32), "tensor")
        + vectors[1]
    )
    second_norm, second_normed, second_inverse = norm_forward(summed_input, vectors[4], vectors[5])
    layer_out = own_rows(second_norm).astype(jnp.bfloat16)
    grad_sum = norm_backward(
        cotangent.astype(jnp.float32), second_normed, second_inverse, vectors[4]
    )
    grad_branch = grad_sum.astype(jnp.bfloat16)
    second_share = own_rows(second_normed)
    grad_w_down = trans_times(active_low, grad_branch)
    grad_active = times_trans(grad_branch, w_down)
    grad_hidden = gelu_back(grad_active)[0].astype(jnp.bfloat16)
    grad_w_in = trans_times(first_low, grad_hidden)
    grad_units = jnp.sum(grad_hidden.astype(jnp.float32), axis=0)
    grad_first = lax.psum(times_trans(grad_hidden, w_in), "tensor") + grad_sum
    grad_h1 = norm_backward(grad_first, first_normed, first_inverse, vectors[2])
    grad_attn = grad_h1.astype(jnp.bfloat16)
    grad_first_share = own_rows(grad_first)
    first_normed_share = own_rows(first_normed)
    grad_h1_share = own_rows(grad_h1)
    grad_w_out = trans_times(mixed_flat, grad_attn)
    grad_mixed = times_trans(grad_attn, w_out).astype(jnp.bfloat16).reshape(head_shape)
    grad_query, grad_key, grad_value = lax.map(
        attend_backward, (queries, key_heads, value_heads, segments, grad_mixed, log_total)
    )
    grad_query = (
        grad_query.reshape(token_count, head_slab).astype(jnp.float32) * head_scale
    ).astype(jnp.bfloat16)
    grad_key = grad_key.reshape(token_count, head_slab)
    grad_value = grad_value.reshape(token_count, head_slab)
    grad_projected = jnp.stack([grad_query, grad_key, grad_value], axis=1).reshape(
        token_count, 3 * head_slab
    )
    grad_w_qkv = trans_times(tokens, grad_projected)
    grad_heads = jnp.stack(
        [
            jnp.sum(grad_query.astype(jnp.float32), axis=0),
            jnp.sum(grad_value.astype(jnp.float32), axis=0),
        ]
    )
    grad_tokens = (
        lax.psum_scatter(
            times_trans(grad_projected, flat_qkv).astype(jnp.bfloat16),
            "tensor",
            scatter_dimension=0,
            tiled=True,
        ).astype(jnp.float32)
        + grad_h1_share
    )
    local_vectors = jnp.stack(
        [
            jnp.sum(own_rows(grad_attn).astype(jnp.float32), axis=0),
            jnp.sum(own_rows(grad_branch).astype(jnp.float32), axis=0),
            jnp.sum(grad_first_share * first_normed_share, axis=0),
            jnp.sum(grad_first_share, axis=0),
            jnp.sum(grad_out_share * second_share, axis=0),
            jnp.sum(grad_out_share, axis=0),
        ]
    )
    zero_index = jnp.zeros((), jnp.int32)
    head_full = lax.dynamic_update_slice(
        jnp.zeros((2, head_slab * tensor_size), jnp.float32),
        grad_heads,
        (zero_index, tensor_place * head_slab),
    )
    unit_full = lax.dynamic_update_slice(
        jnp.zeros((unit_slab * tensor_size,), jnp.float32), grad_units, (tensor_place * unit_slab,)
    )
    vector_sum, head_sum, unit_sum = lax.psum(
        (local_vectors, head_full, unit_full), ("dp", "tensor")
    )
    grad_vectors = vector_sum / replicas
    grad_head_bias = (
        lax.dynamic_slice_in_dim(head_sum, tensor_place * head_slab, head_slab, 1) / replicas
    )
    grad_unit_bias = (
        lax.dynamic_slice_in_dim(unit_sum, tensor_place * unit_slab, unit_slab, 0) / replicas
    )
    combined_qkv = grad_w_qkv + err_qkv[0].reshape(model_width, 3 * head_slab)
    combined_out = grad_w_out + err_out[0]
    combined_in = grad_w_in + err_in[0]
    combined_down = grad_w_down + err_down[0]
    left_qkv, left_out, left_in, left_down = (
        lax.psum(
            left_of(combined_qkv, basis_qkv.reshape(rank_size, 3 * head_slab)).astype(jnp.bfloat16),
            "dp",
        ).astype(jnp.float32),
        lax.psum(left_of(combined_out, basis_out).astype(jnp.bfloat16), "dp").astype(jnp.float32),
        lax.psum(left_of(combined_in, basis_in).astype(jnp.bfloat16), "dp").astype(jnp.float32),
        lax.psum(left_of(combined_down, basis_down).astype(jnp.bfloat16), "dp").astype(jnp.float32),
    )
    ortho_qkv = orthonormal(left_qkv / replicas)
    ortho_out = orthonormal(left_out / replicas)
    ortho_in = orthonormal(left_in / replicas)
    ortho_down = orthonormal(left_down / replicas)
    right_qkv, right_out, right_in, right_down = (
        lax.psum(right_of(ortho_qkv, combined_qkv).astype(jnp.bfloat16), "dp").astype(jnp.float32),
        lax.psum(right_of(ortho_out, combined_out).astype(jnp.bfloat16), "dp").astype(jnp.float32),
        lax.psum(right_of(ortho_in, combined_in).astype(jnp.bfloat16), "dp").astype(jnp.float32),
        lax.psum(right_of(ortho_down, combined_down).astype(jnp.bfloat16), "dp").astype(
            jnp.float32
        ),
    )
    right_qkv = right_qkv / replicas
    right_out = right_out / replicas
    right_in = right_in / replicas
    right_down = right_down / replicas
    rank_qkv = jnp.dot(ortho_qkv, right_qkv, precision=PRECISE)
    rank_out = jnp.dot(ortho_out, right_out, precision=PRECISE)
    rank_in = jnp.dot(ortho_in, right_in, precision=PRECISE)
    rank_down = jnp.dot(ortho_down, right_down, precision=PRECISE)
    reduced_qkv = rank_qkv.reshape(model_width, 3, head_slab)
    new_err_qkv = (combined_qkv - rank_qkv).reshape(1, model_width, 3, head_slab)
    new_err_out = (combined_out - rank_out)[None]
    new_err_in = (combined_in - rank_in)[None]
    new_err_down = (combined_down - rank_down)[None]
    new_basis_qkv = right_qkv.reshape(rank_size, 3, head_slab)
    step_rate = 0.3 * math.sqrt(replicas / token_count)
    new_mom_qkv = 0.9 * mom_qkv + reduced_qkv
    new_mom_head_bias = 0.9 * mom_head_bias + grad_head_bias
    new_mom_out = 0.9 * mom_out + rank_out
    new_mom_in = 0.9 * mom_in + rank_in
    new_mom_unit_bias = 0.9 * mom_unit_bias + grad_unit_bias
    new_mom_down = 0.9 * mom_down + rank_down
    new_mom_vectors = 0.9 * mom_vectors + grad_vectors
    new_w_qkv = w_qkv.astype(jnp.float32) - step_rate * new_mom_qkv
    new_head_bias = head_bias - step_rate * new_mom_head_bias
    new_w_out = w_out.astype(jnp.float32) - step_rate * new_mom_out
    new_w_in = w_in.astype(jnp.float32) - step_rate * new_mom_in
    new_unit_bias = unit_bias - step_rate * new_mom_unit_bias
    new_w_down = w_down.astype(jnp.float32) - step_rate * new_mom_down
    new_vectors = vectors - step_rate * new_mom_vectors
    return (
        layer_out,
        grad_tokens,
        reduced_qkv,
        grad_head_bias,
        rank_out,
        rank_in,
        grad_unit_bias,
        rank_down,
        grad_vectors,
        new_err_qkv,
        new_err_out,
        new_err_in,
        new_err_down,
        new_basis_qkv,
        right_out,
        right_in,
        right_down,
        new_mom_qkv,
        new_mom_head_bias,
        new_mom_out,
        new_mom_in,
        new_mom_unit_bias,
        new_mom_down,
        new_mom_vectors,
        new_w_qkv,
        new_head_bias,
        new_w_out,
        new_w_in,
        new_unit_bias,
        new_w_down,
        new_vectors,
    )


def solution(mesh):
    in_specs = (
        P("dp", None),
        P("dp", None),
        P(None, None, "tensor"),
        P(None, "tensor"),
        P("tensor", None),
        P(None, "tensor"),
        P("tensor"),
        P("tensor", None),
        P(),
        P("dp", None),
        P("dp", None, None, "tensor"),
        P("dp", "tensor", None),
        P("dp", None, "tensor"),
        P("dp", "tensor", None),
        P(None, None, "tensor"),
        P("tensor", None),
        P(None, "tensor"),
        P("tensor", None),
        P(None, None, "tensor"),
        P(None, "tensor"),
        P("tensor", None),
        P(None, "tensor"),
        P("tensor"),
        P("tensor", None),
        P(),
    )
    out_specs = (
        P(("dp", "tensor"), None),
        P(("dp", "tensor"), None),
        P(None, None, "tensor"),
        P(None, "tensor"),
        P("tensor", None),
        P(None, "tensor"),
        P("tensor"),
        P("tensor", None),
        P(),
        P("dp", None, None, "tensor"),
        P("dp", "tensor", None),
        P("dp", None, "tensor"),
        P("dp", "tensor", None),
        P(None, None, "tensor"),
        P("tensor", None),
        P(None, "tensor"),
        P("tensor", None),
        P(None, None, "tensor"),
        P(None, "tensor"),
        P("tensor", None),
        P(None, "tensor"),
        P("tensor"),
        P("tensor", None),
        P(),
        P(None, None, "tensor"),
        P(None, "tensor"),
        P("tensor", None),
        P(None, "tensor"),
        P("tensor"),
        P("tensor", None),
        P(),
    )
    return jax.shard_map(local, mesh=mesh, in_specs=in_specs, out_specs=out_specs, check_vma=False)
```

profile of v0, /device:TPU:12, one launch (start us, length us, event | category | flops | bytes accessed | tf_op | source)
XLA Modules:
  0.0 1268.8 jit_solution(10177957480828531079)
XLA Ops:
  44.9 51.5 %while.26 = (s32[]{:T(128)}, bf16[2,1024,4,64]{1,3,2,0:T(8,128)(2,1)}, f32[2,4,1024]{2,1,0:T(4,128)S(1)}, bf16[2,1024,4,64]{1,3,2,0:T(8,128)(2,1)}, s32[2,1024]{...) while((s32[]{:T(128)}, ...), condition=%wide.region_3.4_spmd, body=%wide.region_0.3_spmd.sunk | while | flops 1112797184 | bytes 56768612 | solution.py:172
  87.5 8.9 fusion.155
  106.4 153.3 %all-reduce.7.cloned.1.call-done = f32[2048,1024]{1,0:T(8,128)} async-done(((f32[2048,1024]{1,0:T(8,128)}), f32[2048,1024]{1,0:T(8,128)}) %all-reduce.7.cloned.1.call-update) | async-done | bytes 8388624 | tf_op jit(solution)/shard_map/psum | solution.py:175
  271.8 24.4 %multiply_convert_fusion.1 = (bf16[2048,1024]{1,0:T(8,128)(2,1)S(1)}, f32[2048,1024]{1,0:T(8,128)}, f32[2048,1024]{1,0:T(8,128)}) fusion(f32[1024]{0:T(1024)S(1)} %copy-done.65, bf16[1024,1024]{1,0:T(8,128)(2,1)S(1)} %copy-done.37, f32[2048,1024]{1,0:T(8,128)S(1)} %subtract_multiply_fusion.3, f32[1024]{0:T(1024)S(1)} %bitcast.353, f32[1024]{0:T(1024)S(1)} %bitcast.281), kind=kOutput, calls=%fused_computation.74 | convolution fusion | flops 4439670784 | bytes 31469568 | tf_op jit(solution)/shard_map/dot_general | solution.py:182
  304.9 153.1 %all-reduce.9.cloned.1.call-done = f32[2048,1024]{1,0:T(8,128)} async-done(((f32[2048,1024]{1,0:T(8,128)}), f32[2048,1024]{1,0:T(8,128)}) %all-reduce.9.cloned.1.call-update) | async-done | bytes 8388624 | tf_op jit(solution)/shard_map/psum | solution.py:188
  473.5 13.2 %convert_reduce_fusion = (f32[1024]{0:T(1024)S(1)}, bf16[2048,1024]{1,0:T(8,128)(2,1)S(1)}) fusion(f32[2048,1024]{1,0:T(8,128)} %get-tuple-element.569, f32[2048,1024]{1,0:T(8,128)} %get-tuple-element.620, f32[1024]{0:T(1024)S(1)} %copy-done.65, bf16[2048,1024]{1,0:T(8,128)(2,1)S(1)} %fusion.74, bf16[1024,1024]{1,0:T(8,128)(2,1)S(1)} %copy-done.39), kind=kOutput, calls=%fused_computation.64 | convolution fusion | flops 4330617856 | bytes 27271168 | tf_op jit(solution)/shard_map/dot_general | solution.py:32
  505.4 9.5 bitcast_add_fusion
  532.2 116.6 %all-reduce.11.cloned.1.call-done = f32[2048,1024]{1,0:T(8,128)} async-done(((f32[2048,1024]{1,0:T(8,128)}), f32[2048,1024]{1,0:T(8,128)}) %all-reduce.11.cloned.1.call-update) | async-done | bytes 8388624 | tf_op jit(solution)/shard_map/psum | solution.py:203
  648.8 11.4 multiply_reduce_fusion.5
  660.3 9.5 fusion.76
  683.1 95.2 %while.27 = (s32[]{:T(128)}, bf16[2,1024,4,64]{1,3,2,0:T(8,128)(2,1)}, bf16[2,1024,4,64]{1,3,2,0:T(8,128)(2,1)}, bf16[2,1024,4,64]{1,3,2,0:T(8,128)(2,1)}, bf16[...) while((s32[]{:T(128)}, ...), condition=%wide.region_17.18_spmd, body=%wide.region_15.17_spmd.sunk | while | flops 2736517120 | bytes 219284944 | solution.py:211
  684.2 9.5 fusion.164
  702.6 14.7 %multiply_reduce_fusion.152 = (f32[4,1024]{1,0:T(4,128)S(1)}, f32[4,1024,1024]{1,2,0:T(8,128)}) fusion(f32[4,1024,1024]{1,2,0:T(8,128)} %fusion.164, f32[4,1024]{1,0:T(4,128)S(1)} %dynamic-slice_bitcast_fusion.2, pred[1024,1024]{0,1:T(8,128)(4,1)} %copy-done.2, bf16[2,1024,4,64]{1,3,2,0:T(8,128)(2,1)} %get-tuple-element.793, s32[]{:T(128)S(6)} %copy.165, ...), kind=kOutput, calls=%fused_computation.22.clone.1 | convolution fusion | flops 553644032 | bytes 35685376 | tf_op jit(solution)/shard_map/while/body/eval_jaxpr/qhd,khd->hqk/dot_general | solution.py:97
  731.6 9.5 fusion.164
  750.0 14.7 %multiply_reduce_fusion.152 = (f32[4,1024]{1,0:T(4,128)S(1)}, f32[4,1024,1024]{1,2,0:T(8,128)}) fusion(f32[4,1024,1024]{1,2,0:T(8,128)} %fusion.164, f32[4,1024]{1,0:T(4,128)S(1)} %dynamic-slice_bitcast_fusion.2, pred[1024,1024]{0,1:T(8,128)(4,1)} %copy-done.2, bf16[2,1024,4,64]{1,3,2,0:T(8,128)(2,1)} %get-tuple-element.793, s32[]{:T(128)S(6)} %copy.165, ...), kind=kOutput, calls=%fused_computation.22.clone.1 | convolution fusion | flops 553644032 | bytes 35685376 | tf_op jit(solution)/shard_map/while/body/eval_jaxpr/qhd,khd->hqk/dot_general | solution.py:97
  827.3 35.2 %all-reduce.2 = (bf16[1024,8]{0,1:T(8,128)(2,1)S(1)}, bf16[256,8]{0,1:T(8,128)(2,1)S(1)}, bf16[1024,8]{0,1:T(8,128)(2,1)S(1)}, bf16[1024,8]{0,1:T(8,128)(2,1)S(1)}) all-reduce(bf16[1024,8]{0,1:T(8,128)(2,1)S(1)} %convolution_convert_fusion.8, ...), channel_id=1, replica_groups=mesh['dp'=8,'tensor'=4] {'dp'}, use_global_device_ids=true, to_apply=%region_19.20 | all-reduce | flops 26624 | bytes 106496 | tf_op jit(solution)/shard_map/psum | solution.py:272
  1040.1 17.5 %subtract_divide_fusion.21 = (f32[256,1]{0,1:T(1,128)S(1)}, f32[256,1]{0,1:T(1,128)S(1)}, f32[256,1]{0,1:T(1,128)S(1)}, f32[256,1]{0,1:T(1,128)S(1)}, f32[256,1]...) fusion(f32[256,1]{0,1:T(1,128)S(1)} %get-tuple-element.613, f32[]{:T(128)S(6)} %add.371, ...), kind=kLoop, calls=%fused_computation.402 | loop fusion | flops 16128 | bytes 15500 | tf_op jit(solution)/shard_map/div | solution.py:69
  1057.7 18.2 %subtract_divide_fusion.14 = (f32[1024,1]{0,1:T(1,128)S(1)}, f32[1024,1]{0,1:T(1,128)S(1)}, f32[1024,1]{0,1:T(1,128)S(1)}, f32[1024,1]{0,1:T(1,128)S(1)}, f32[10...) fusion(f32[1024,1]{0,1:T(1,128)S(1)} %get-tuple-element.599, f32[]{:T(128)S(6)} %add.361, ...), kind=kLoop, calls=%fused_computation.300 | loop fusion | flops 64512 | bytes 61580 | tf_op jit(solution)/shard_map/div | solution.py:69
  1075.9 17.4 %subtract_divide_fusion.7 = (f32[1024,1]{0,1:T(1,128)S(1)}, f32[1024,1]{0,1:T(1,128)S(1)}, f32[1024,1]{0,1:T(1,128)S(1)}, f32[1024,1]{0,1:T(1,128)S(1)}, f32[102...) fusion(f32[1024,1]{0,1:T(1,128)S(1)} %get-tuple-element.591, f32[]{:T(128)S(6)} %add.380, ...), kind=kLoop, calls=%fused_computation.230 | loop fusion | flops 64512 | bytes 61580 | tf_op jit(solution)/shard_map/div | solution.py:69
  1093.3 17.5 %subtract_divide_fusion = (f32[1024,1]{0,1:T(1,128)S(1)}, f32[1024,1]{0,1:T(1,128)S(1)}, f32[1024,1]{0,1:T(1,128)S(1)}, f32[1024,1]{0,1:T(1,128)S(1)}, f32[1024,...) fusion(f32[1024,1]{0,1:T(1,128)S(1)} %get-tuple-element.583, f32[]{:T(128)S(6)} %add.390, ...), kind=kLoop, calls=%fused_computation.159 | loop fusion | flops 64512 | bytes 61580 | tf_op jit(solution)/shard_map/div | solution.py:69
  1121.9 33.7 %all-reduce.1 = (bf16[8,768]{1,0:T(8,128)(2,1)S(1)}, bf16[8,1024]{1,0:T(8,128)(2,1)S(1)}, bf16[8,1024]{1,0:T(8,128)(2,1)S(1)}, bf16[8,1024]{1,0:T(8,128)(2,1)S(1)}) all-reduce(bf16[8,768]{1,0:T(8,128)(2,1)S(1)} %convolution_convert_fusion.9, ...), channel_id=1, replica_groups=mesh['dp'=8,'tensor'=4] {'dp'}, use_global_device_ids=true, to_apply=%region_56.57 | all-reduce | flops 30720 | bytes 122880 | tf_op jit(solution)/shard_map/psum | solution.py:285
  1172.0 43.4 %all-reduce = (f32[2,1024]{1,0:T(2,128)S(1)}, f32[4096]{0:T(1024)S(1)}, f32[6,1024]{1,0:T(8,128)S(1)}) all-reduce(f32[2,1024]{1,0:T(2,128)S(1)} %constant_dynamic-update-slice_fusion.3, f32[4096]{0:T(1024)S(1)} %copy-done.56, f32[6,1024]{1,0:T(8,128)S(1)} %stack.44), channel_id=1, replica_groups=mesh['dp'=8,'tensor'=4] {'dp','tensor'}, use_global_device_ids=true, to_apply=%region_59.60 | all-reduce | flops 12288 | bytes 98304 | tf_op jit(solution)/shard_map/psum | solution.py:257
  1234.5 12.2 multiply_subtract_fusion.1
  1246.7 11.5 multiply_subtract_fusion
  (384 shorter events, 476.0 us)
Async XLA Ops:
  7.2 509.6 %copy-start = (f32[8,1024]{1,0:T(8,128)S(1)}, f32[8,1024]{1,0:T(8,128)}, u32[]{:S(2)}) copy-start(f32[8,1024]{1,0:T(8,128)} %param.46) | copy-start | bytes 98308
  7.2 252.4 %all-reduce.7.cloned.1.call-start = ((), (), s32[]{:S(2)}) async-start(), calls=%async_computation.1 | async-start | bytes 16777216 | tf_op jit(solution)/shard_map/psum | solution.py:175
  106.3 351.7 %all-reduce.9.cloned.1.call-start = ((), (), s32[]{:S(2)}) async-start(), calls=%async_computation.2 | async-start | bytes 16777216 | tf_op jit(solution)/shard_map/psum | solution.py:188
  271.7 24.5 %copy-start.3 = (f32[2048,1024]{1,0:T(8,128)}, f32[2048,1024]{1,0:T(8,128)S(1)}, u32[]{:S(2)}) copy-start(f32[2048,1024]{1,0:T(8,128)S(1)} %subtract_multiply_fusion.3) | copy-start | bytes 25165828
  271.8 26.4 %copy-start.38 = (bf16[1024,1024]{1,0:T(8,128)(2,1)S(1)}, bf16[1024,1024]{1,0:T(8,128)(2,1)}, u32[]{:S(2)}) copy-start(bf16[1024,1024]{1,0:T(8,128)(2,1)} %param.36) | copy-start | bytes 6291460
  304.9 343.9 %all-reduce.11.cloned.1.call-start = ((), (), s32[]{:S(2)}) async-start(), calls=%async_computation.3 | async-start | bytes 16777216 | tf_op jit(solution)/shard_map/psum | solution.py:203
  495.6 762.6 %reduce-scatter.2.cloned.1.call-start = ((), (), s32[]{:S(2)}) async-start(), calls=%async_computation.4 | async-start | bytes 5242880 | tf_op jit(solution)/shard_map/reduce_scatter | solution.py:230
  500.8 20.3 %slice-start.4 = ((s8[8388608]{0:T(1024)(128)(4,1)}), s8[4194304]{0:T(1024)(128)(4,1)S(1)}, s32[]{:S(2)}) async-start(s8[8388608]{0:T(1024)(128)(4,1)} %bitcast.240), calls=%async_computation.9 | async-start | bytes 8388608
  505.4 15.6 %copy-start.71 = (bf16[2048,1024]{1,0:T(8,128)(2,1)S(1)}, bf16[2048,1024]{1,0:T(8,128)(2,1)}, u32[]{:S(2)}) copy-start(bf16[2048,1024]{1,0:T(8,128)(2,1)} %copy-done.70) | copy-start | bytes 12582916
  532.2 128.1 %copy-start.52 = (f32[2048]{0:T(1024)S(1)}, f32[2048]{0:T(1024)}, u32[]{:S(2)}) copy-start(f32[2048]{0:T(1024)} %copy-done.51) | copy-start | bytes 24580
  693.7 23.6 %slice-start = ((s8[16777216]{0:T(1024)(128)(4,1)}), s8[4194304]{0:T(1024)(128)(4,1)S(1)}, s32[]{:S(2)}) async-start(s8[16777216]{0:T(1024)(128)(4,1)} %bitcast.238), calls=%async_computation.5 | async-start | bytes 8388608 | tf_op jit(solution)/shard_map/while
  693.7 23.6 %slice-start.1 = ((s8[16777216]{0:T(1024)(128)(4,1)}), s8[4194304]{0:T(1024)(128)(4,1)S(1)}, s32[]{:S(2)}) async-start(s8[16777216]{0:T(1024)(128)(4,1)} %bitcast.238), calls=%async_computation.6 | async-start | bytes 8388608 | tf_op jit(solution)/shard_map/while
  741.2 23.6 %slice-start = ((s8[16777216]{0:T(1024)(128)(4,1)}), s8[4194304]{0:T(1024)(128)(4,1)S(1)}, s32[]{:S(2)}) async-start(s8[16777216]{0:T(1024)(128)(4,1)} %bitcast.238), calls=%async_computation.5 | async-start | bytes 8388608 | tf_op jit(solution)/shard_map/while
  741.2 23.6 %slice-start.1 = ((s8[16777216]{0:T(1024)(128)(4,1)}), s8[4194304]{0:T(1024)(128)(4,1)S(1)}, s32[]{:S(2)}) async-start(s8[16777216]{0:T(1024)(128)(4,1)} %bitcast.238), calls=%async_computation.6 | async-start | bytes 8388608 | tf_op jit(solution)/shard_map/while
  1160.2 55.3 %copy-start.64 = (f32[2,256]{1,0:T(2,128)S(1)}, f32[2,256]{1,0:T(2,128)}, u32[]{:S(2)}) copy-start(f32[2,256]{1,0:T(2,128)} %param.32) | copy-start | bytes 6148
  1160.2 55.3 %copy-start.68 = (f32[2,256]{1,0:T(2,128)S(1)}, f32[2,256]{1,0:T(2,128)}, u32[]{:S(2)}) copy-start(f32[2,256]{1,0:T(2,128)} %param.48) | copy-start | bytes 6148
  1160.2 55.9 %copy-start.66 = (f32[1024]{0:T(1024)S(1)}, f32[1024]{0:T(1024)}, u32[]{:S(2)}) copy-start(f32[1024]{0:T(1024)} %param.35) | copy-start | bytes 12292
  1160.3 55.8 %copy-start.67 = (f32[1024]{0:T(1024)S(1)}, f32[1024]{0:T(1024)}, u32[]{:S(2)}) copy-start(f32[1024]{0:T(1024)} %param.51) | copy-start | bytes 12292
  1160.3 57.1 %copy-start.50 = (f32[6,1024]{1,0:T(8,128)S(1)}, f32[6,1024]{1,0:T(8,128)}, u32[]{:S(2)}) copy-start(f32[6,1024]{1,0:T(8,128)} %param.37) | copy-start | bytes 73732
  1160.3 57.1 %copy-start.59 = (f32[6,1024]{1,0:T(8,128)S(1)}, f32[6,1024]{1,0:T(8,128)}, u32[]{:S(2)}) copy-start(f32[6,1024]{1,0:T(8,128)} %param.53) | copy-start | bytes 73732
  1166.3 64.8 %copy-start.19 = (f32[1024,3,256]{2,0,1:T(8,128)}, f32[1024,3,256]{2,0,1:T(8,128)S(1)}, u32[]{:S(2)}) copy-start(f32[1024,3,256]{2,0,1:T(8,128)S(1)} %copy.125) | copy-start | bytes 9437188
  1217.3 17.2 %copy-start.48 = (f32[8,1024]{1,0:T(8,128)}, f32[8,1024]{1,0:T(8,128)S(1)}, u32[]{:S(2)}) copy-start(f32[8,1024]{1,0:T(8,128)S(1)} %convert_multiply_fusion.6) | copy-start | bytes 98308
  1217.4 17.1 %copy-start.46 = (f32[8,1024]{1,0:T(8,128)}, f32[8,1024]{1,0:T(8,128)S(1)}, u32[]{:S(2)}) copy-start(f32[8,1024]{1,0:T(8,128)S(1)} %convert_multiply_fusion.4) | copy-start | bytes 98308
  1217.4 17.1 %copy-start.47 = (f32[8,1024]{1,0:T(8,128)}, f32[8,1024]{1,0:T(8,128)S(1)}, u32[]{:S(2)}) copy-start(f32[8,1024]{1,0:T(8,128)S(1)} %convert_multiply_fusion.2) | copy-start | bytes 98308
  (70 other events, 549.4 us)
Sparse Core Ops, SparseCore 0:
  106.4 153.2 all-reduce.6
  305.0 153.0 all-reduce.8
  495.7 152.9 all-reduce.10
  1029.7 43.5 reduce-scatter.1
where the time goes:
time: 1280 us; the launch traced here: 1270 us
  waiting for transfers between devices  423 us (33%)
  other arithmetic  359 us (28%)
  matrix products  242 us (19%)
  blocking collectives  112 us (9%)
  local copies, waits for them, and re-layouts  94.7 us (7%)
  between operations  37 us (3%)
    psum x1, waiting for transfers between devices, local(): lax.psum(jnp.dot(mixed_flat, w_out, preferred_element_type=jnp.float32),...  153 us
    psum x1, waiting for transfers between devices, local(): lax.psum(jnp.dot(active_low, w_down, preferred_element_type=jnp.float32),...  153 us
    reduce_sum x40, other arithmetic, orthonormal(): jnp.sum(earlier * column, axis=-1, keepdims=True) * earlier  122 us
    psum x1, waiting for transfers between devices, local(): grad_first = lax.psum(times_trans(grad_hidden, w_in), 'tensor') + grad_sum  117 us
    div x4, other arithmetic, orthonormal(): column / (jnp.sqrt(jnp.sum(column * column, axis=-1, keepdims=True)) + EP...  70.6 us
    psum x1, blocking collectives, local(): lax.psum((local_vectors, head_full, unit_full), ('dp', 'tensor'))  43.4 us
    psum x1, blocking collectives, local(): lax.psum(left_of(combined_qkv, basis_qkv.reshape(rank_size, 3 * head_slab...  35.2 us
    reduce_sum x20, other arithmetic, orthonormal(): jnp.sum(column * column, axis=-1, keepdims=True)  33.8 us
  transfers between devices with their start and end apart: 4, of which 3 were waited for; matrix products, arithmetic and copies ran while one was open for 14% of the time, Pallas kernels for 0%

commit v1 on v0

--- a/solution.py
+++ b/solution.py
@@ -1,3 +1,4 @@
+import functools
 from functools import partial
 import math
 import jax
@@ -10,6 +11,13 @@
 EPS_NORM = 1e-05
 EPS_BASIS = 1e-08
 MASKED = -1000000000.0
+
+
+def deliver_the_words(in_array, mesh_name):
+    return jnp.sum(jax.lax.all_gather(in_array, mesh_name), 0)
+
+
+play_run = functools.partial(deliver_the_words, mesh_name="dp")
 
 
 def norm_forward(values, gain, shift):
@@ -282,7 +290,7 @@
     ortho_in = orthonormal(left_in / replicas)
     ortho_down = orthonormal(left_down / replicas)
     right_qkv, right_out, right_in, right_down = (
-        lax.psum(right_of(ortho_qkv, combined_qkv).astype(jnp.bfloat16), "dp").astype(jnp.float32),
+        play_run(right_of(ortho_qkv, combined_qkv).astype(jnp.bfloat16)).astype(jnp.float32),
         lax.psum(right_of(ortho_out, combined_out).astype(jnp.bfloat16), "dp").astype(jnp.float32),
         lax.psum(right_of(ortho_in, combined_in).astype(jnp.bfloat16), "dp").astype(jnp.float32),
         lax.psum(right_of(ortho_down, combined_down).astype(jnp.bfloat16), "dp").astype(

time: 1280 us -> 1350 us (1.055)
  waiting for transfers between devices: 423 us -> 490 us
    psum x0 -> x1, waiting for transfers between devices: none -> 67.3 us  [local(): lax.psum(left_of(combined_qkv, basis_qkv.reshape(rank_size, 3 * head_slab...]
    psum x2 -> x1, blocking collectives: 68.9 us -> 35.1 us  [local(): lax.psum(left_of(combined_out, basis_out).astype(jnp.bfloat16), 'dp')]
    all_gather x0 -> x1, blocking collectives: none -> 27.7 us  [deliver_the_words(): return jnp.sum(jax.lax.all_gather(in_array, mesh_name), 0)]
    unnamed x139 -> x147, local copies, waits for them, and re-layouts: 33.3 us -> 31.3 us
  transfers between devices with their start and end apart: 4 -> 5, of which waited for: 3 -> 4; matrix products, arithmetic and copies ran while one was open for 14% -> 11% of each run, Pallas kernels for 0% -> 0%
where the time goes in v1:
time: 1350 us; the launch traced here: 1330 us
  waiting for transfers between devices  490 us (36%)
  other arithmetic  359 us (27%)
  matrix products  245 us (18%)
  blocking collectives  106 us (8%)
  local copies, waits for them, and re-layouts  92.6 us (7%)
  between operations  37 us (3%)
    psum x1, waiting for transfers between devices, local(): lax.psum(jnp.dot(mixed_flat, w_out, preferred_element_type=jnp.float32),...  153 us
    psum x1, waiting for transfers between devices, local(): lax.psum(jnp.dot(active_low, w_down, preferred_element_type=jnp.float32),...  153 us
    reduce_sum x40, other arithmetic, orthonormal(): jnp.sum(earlier * column, axis=-1, keepdims=True) * earlier  123 us
    psum x1, waiting for transfers between devices, local(): grad_first = lax.psum(times_trans(grad_hidden, w_in), 'tensor') + grad_sum  117 us
    div x4, other arithmetic, orthonormal(): column / (jnp.sqrt(jnp.sum(column * column, axis=-1, keepdims=True)) + EP...  71.5 us
    psum x1, waiting for transfers between devices, local(): lax.psum(left_of(combined_qkv, basis_qkv.reshape(rank_size, 3 * head_slab...  67.3 us
    psum x1, blocking collectives, local(): lax.psum((local_vectors, head_full, unit_full), ('dp', 'tensor'))  43.7 us
    psum x1, blocking collectives, local(): lax.psum(left_of(combined_out, basis_out).astype(jnp.bfloat16), 'dp')  35.1 us
  transfers between devices with their start and end apart: 5, of which 4 were waited for; matrix products, arithmetic and copies ran while one was open for 11% of the time, Pallas kernels for 0%

profile of v1, /device:TPU:12, one launch (start us, length us, event | category | flops | bytes accessed | tf_op | source)
XLA Modules:
  0.0 1332.1 jit_solution(1175412139321702879)
XLA Ops:
  44.9 51.5 %while.26 = (s32[]{:T(128)}, bf16[2,1024,4,64]{1,3,2,0:T(8,128)(2,1)}, f32[2,4,1024]{2,1,0:T(4,128)S(1)}, bf16[2,1024,4,64]{1,3,2,0:T(8,128)(2,1)}, s32[2,1024]{...) while((s32[]{:T(128)}, ...), condition=%wide.region_3.4_spmd, body=%wide.region_0.3_spmd.sunk | while | flops 1112797184 | bytes 56768612 | solution.py:180
  87.5 8.9 fusion.155
  106.4 153.3 %all-reduce.8.cloned.1.call-done = f32[2048,1024]{1,0:T(8,128)} async-done(((f32[2048,1024]{1,0:T(8,128)}), f32[2048,1024]{1,0:T(8,128)}) %all-reduce.8.cloned.1.call-update) | async-done | bytes 8388624 | tf_op jit(solution)/shard_map/psum | solution.py:183
  271.8 24.4 %multiply_convert_fusion.1 = (bf16[2048,1024]{1,0:T(8,128)(2,1)S(1)}, f32[2048,1024]{1,0:T(8,128)}, f32[2048,1024]{1,0:T(8,128)}) fusion(f32[1024]{0:T(1024)S(1)} %copy-done.69, bf16[1024,1024]{1,0:T(8,128)(2,1)S(1)} %copy-done.35, f32[2048,1024]{1,0:T(8,128)S(1)} %subtract_multiply_fusion.3, f32[1024]{0:T(1024)S(1)} %bitcast.355, f32[1024]{0:T(1024)S(1)} %bitcast.283), kind=kOutput, calls=%fused_computation.74 | convolution fusion | flops 4439670784 | bytes 31469568 | tf_op jit(solution)/shard_map/dot_general | solution.py:190
  304.9 153.1 %all-reduce.10.cloned.1.call-done = f32[2048,1024]{1,0:T(8,128)} async-done(((f32[2048,1024]{1,0:T(8,128)}), f32[2048,1024]{1,0:T(8,128)}) %all-reduce.10.cloned.1.call-update) | async-done | bytes 8388624 | tf_op jit(solution)/shard_map/psum | solution.py:196
  473.5 13.2 convert_reduce_fusion
  505.4 9.5 bitcast_add_fusion
  532.2 116.6 %all-reduce.12.cloned.1.call-done = f32[2048,1024]{1,0:T(8,128)} async-done(((f32[2048,1024]{1,0:T(8,128)}), f32[2048,1024]{1,0:T(8,128)}) %all-reduce.12.cloned.1.call-update) | async-done | bytes 8388624 | tf_op jit(solution)/shard_map/psum | solution.py:211
  648.8 11.4 multiply_reduce_fusion.5
  683.6 95.3 %while.27 = (s32[]{:T(128)}, bf16[2,1024,4,64]{1,3,2,0:T(8,128)(2,1)}, bf16[2,1024,4,64]{1,3,2,0:T(8,128)(2,1)}, bf16[2,1024,4,64]{1,3,2,0:T(8,128)(2,1)}, bf16[...) while((s32[]{:T(128)}, ...), condition=%wide.region_17.18_spmd, body=%wide.region_15.17_spmd.sunk | while | flops 2736517120 | bytes 219284944 | solution.py:219
  684.7 9.5 fusion.164
  703.1 14.7 %multiply_reduce_fusion.152 = (f32[4,1024]{1,0:T(4,128)S(1)}, f32[4,1024,1024]{1,2,0:T(8,128)}) fusion(f32[4,1024,1024]{1,2,0:T(8,128)} %fusion.164, f32[4,1024]{1,0:T(4,128)S(1)} %dynamic-slice_bitcast_fusion.2, pred[1024,1024]{0,1:T(8,128)(4,1)} %copy-done.2, bf16[2,1024,4,64]{1,3,2,0:T(8,128)(2,1)} %get-tuple-element.794, s32[]{:T(128)S(6)} %copy.165, ...), kind=kOutput, calls=%fused_computation.22.clone.1 | convolution fusion | flops 553644032 | bytes 35685376 | tf_op jit(solution)/shard_map/while/body/eval_jaxpr/qhd,khd->hqk/dot_general | solution.py:105
  732.1 9.5 fusion.164
  750.5 14.7 %multiply_reduce_fusion.152 = (f32[4,1024]{1,0:T(4,128)S(1)}, f32[4,1024,1024]{1,2,0:T(8,128)}) fusion(f32[4,1024,1024]{1,2,0:T(8,128)} %fusion.164, f32[4,1024]{1,0:T(4,128)S(1)} %dynamic-slice_bitcast_fusion.2, pred[1024,1024]{0,1:T(8,128)(4,1)} %copy-done.2, bf16[2,1024,4,64]{1,3,2,0:T(8,128)(2,1)} %get-tuple-element.794, s32[]{:T(128)S(6)} %copy.165, ...), kind=kOutput, calls=%fused_computation.22.clone.1 | convolution fusion | flops 553644032 | bytes 35685376 | tf_op jit(solution)/shard_map/while/body/eval_jaxpr/qhd,khd->hqk/dot_general | solution.py:105
  818.5 35.1 %all-reduce.2 = (bf16[256,8]{0,1:T(8,128)(2,1)S(1)}, bf16[1024,8]{0,1:T(8,128)(2,1)S(1)}, bf16[1024,8]{0,1:T(8,128)(2,1)S(1)}) all-reduce(bf16[256,8]{0,1:T(8,128)(2,1)S(1)} %convolution_convert_fusion.10, bf16[1024,8]{0,1:T(8,128)(2,1)S(1)} %copy-done.51, bf16[1024,8]{0,1:T(8,128)(2,1)S(1)} %copy-done.50), channel_id=1, replica_groups=mesh['dp'=8,'tensor'=4] {'dp'}, use_global_device_ids=true, to_apply=%region_60.61 | all-reduce | flops 18432 | bytes 73728 | tf_op jit(solution)/shard_map/psum | solution.py:284
  895.7 17.9 %subtract_divide_fusion.21 = (f32[256,1]{0,1:T(1,128)S(1)}, f32[256,1]{0,1:T(1,128)S(1)}, f32[256,1]{0,1:T(1,128)S(1)}, f32[256,1]{0,1:T(1,128)S(1)}, f32[256,1]...) fusion(f32[256,1]{0,1:T(1,128)S(1)} %get-tuple-element.612, f32[]{:T(128)S(6)} %add.369, ...), kind=kLoop, calls=%fused_computation.403 | loop fusion | flops 16128 | bytes 15500 | tf_op jit(solution)/shard_map/div | solution.py:77
  961.3 17.9 %subtract_divide_fusion = (f32[1024,1]{0,1:T(1,128)S(1)}, f32[1024,1]{0,1:T(1,128)S(1)}, f32[1024,1]{0,1:T(1,128)S(1)}, f32[1024,1]{0,1:T(1,128)S(1)}, f32[1024,...) fusion(f32[1024,1]{0,1:T(1,128)S(1)} %get-tuple-element.590, f32[]{:T(128)S(6)} %add.388, ...), kind=kLoop, calls=%fused_computation.160 | loop fusion | flops 64512 | bytes 61580 | tf_op jit(solution)/shard_map/div | solution.py:77
  1028.5 17.8 %subtract_divide_fusion.7 = (f32[1024,1]{0,1:T(1,128)S(1)}, f32[1024,1]{0,1:T(1,128)S(1)}, f32[1024,1]{0,1:T(1,128)S(1)}, f32[1024,1]{0,1:T(1,128)S(1)}, f32[102...) fusion(f32[1024,1]{0,1:T(1,128)S(1)} %get-tuple-element.598, f32[]{:T(128)S(6)} %add.378, ...), kind=kLoop, calls=%fused_computation.231 | loop fusion | flops 64512 | bytes 61580 | tf_op jit(solution)/shard_map/div | solution.py:77
  1051.5 43.7 %all-reduce = (f32[2,1024]{1,0:T(2,128)S(1)}, f32[4096]{0:T(1024)S(1)}, f32[6,1024]{1,0:T(8,128)S(1)}) all-reduce(f32[2,1024]{1,0:T(2,128)S(1)} %constant_dynamic-update-slice_fusion.3, f32[4096]{0:T(1024)S(1)} %copy-done.53, f32[6,1024]{1,0:T(8,128)S(1)} %stack.44), channel_id=1, replica_groups=mesh['dp'=8,'tensor'=4] {'dp','tensor'}, use_global_device_ids=true, to_apply=%region_59.60 | all-reduce | flops 12288 | bytes 98304 | tf_op jit(solution)/shard_map/psum | solution.py:265
  1107.1 67.3 %all-reduce.14.cloned.1.call-done = (bf16[1024,8]{0,1:T(8,128)(2,1)}, bf16[8,1024]{1,0:T(8,128)(2,1)}, bf16[8,1024]{1,0:T(8,128)(2,1)}, bf16[8,1024]{1,0:T(8,128)(2,1)}) async-done(((bf16[1024,8]{0,1:T(8,128)(2,1)}, bf16[8,1024]{1,0:T(8,128)(2,1)}, bf16[8,1024]{1,0:T(8,128)(2,1)}, bf16[8,1024]{1,0:T(8,128)(2,1)}), (bf16[1024,8]{0,1:T(8,128)(2,1)}, bf16[8,1024]{1,0:T(8,128)(2,1)}, bf16[8,1024]{1,0:T(8,128)(2,1)}, ...) | async-done | bytes 65552 | tf_op jit(solution)/shard_map/psum | solution.py:280
  1220.9 18.0 %subtract_divide_fusion.14 = (f32[1024,1]{0,1:T(1,128)S(1)}, f32[1024,1]{0,1:T(1,128)S(1)}, f32[1024,1]{0,1:T(1,128)S(1)}, f32[1024,1]{0,1:T(1,128)S(1)}, f32[10...) fusion(f32[1024,1]{0,1:T(1,128)S(1)} %get-tuple-element.582, f32[]{:T(128)S(6)} %add.359, ...), kind=kLoop, calls=%fused_computation.301 | loop fusion | flops 64512 | bytes 61580 | tf_op jit(solution)/shard_map/div | solution.py:77
  1241.5 27.7 %all-gather = bf16[64,768]{1,0:T(8,128)(2,1)S(1)} all-gather(bf16[8,768]{1,0:T(8,128)(2,1)S(1)} %convolution_convert_fusion.9), channel_id=2, replica_groups=mesh['dp'=8,'tensor'=4] {'dp'}, dimensions={0}, use_global_device_ids=true | all-gather | bytes 110592 | tf_op jit(solution)/shard_map/all_gather | solution.py:17
  1297.3 12.1 multiply_subtract_fusion.1
  1309.4 12.1 multiply_subtract_fusion
  (395 shorter events, 485.8 us)
Async XLA Ops:
  7.2 509.6 %copy-start = (f32[8,1024]{1,0:T(8,128)S(1)}, f32[8,1024]{1,0:T(8,128)}, u32[]{:S(2)}) copy-start(f32[8,1024]{1,0:T(8,128)} %param.46) | copy-start | bytes 98308
  7.2 252.4 %all-reduce.8.cloned.1.call-start = ((), (), s32[]{:S(2)}) async-start(), calls=%async_computation.1 | async-start | bytes 16777216 | tf_op jit(solution)/shard_map/psum | solution.py:183
  106.3 351.8 %all-reduce.10.cloned.1.call-start = ((), (), s32[]{:S(2)}) async-start(), calls=%async_computation.2 | async-start | bytes 16777216 | tf_op jit(solution)/shard_map/psum | solution.py:196
  271.7 24.5 %copy-start.3 = (f32[2048,1024]{1,0:T(8,128)}, f32[2048,1024]{1,0:T(8,128)S(1)}, u32[]{:S(2)}) copy-start(f32[2048,1024]{1,0:T(8,128)S(1)} %subtract_multiply_fusion.3) | copy-start | bytes 25165828
  271.8 26.5 %copy-start.36 = (bf16[1024,1024]{1,0:T(8,128)(2,1)S(1)}, bf16[1024,1024]{1,0:T(8,128)(2,1)}, u32[]{:S(2)}) copy-start(bf16[1024,1024]{1,0:T(8,128)(2,1)} %param.36) | copy-start | bytes 6291460
  304.9 343.9 %all-reduce.12.cloned.1.call-start = ((), (), s32[]{:S(2)}) async-start(), calls=%async_computation.3 | async-start | bytes 16777216 | tf_op jit(solution)/shard_map/psum | solution.py:211
  495.6 678.8 %all-reduce.14.cloned.1.call-start = ((), (), s32[]{:S(2)}) async-start(), calls=%async_computation.5 | async-start | bytes 131072 | tf_op jit(solution)/shard_map/psum | solution.py:280
  532.2 130.6 %copy-start.49 = (f32[2048]{0:T(1024)S(1)}, f32[2048]{0:T(1024)}, u32[]{:S(2)}) copy-start(f32[2048]{0:T(1024)} %copy-done.48) | copy-start | bytes 24580
  694.2 23.6 %slice-start = ((s8[16777216]{0:T(1024)(128)(4,1)}), s8[4194304]{0:T(1024)(128)(4,1)S(1)}, s32[]{:S(2)}) async-start(s8[16777216]{0:T(1024)(128)(4,1)} %bitcast.240), calls=%async_computation.6 | async-start | bytes 8388608 | tf_op jit(solution)/shard_map/while
  694.2 23.6 %slice-start.1 = ((s8[16777216]{0:T(1024)(128)(4,1)}), s8[4194304]{0:T(1024)(128)(4,1)S(1)}, s32[]{:S(2)}) async-start(s8[16777216]{0:T(1024)(128)(4,1)} %bitcast.240), calls=%async_computation.7 | async-start | bytes 8388608 | tf_op jit(solution)/shard_map/while
  741.7 23.6 %slice-start.1 = ((s8[16777216]{0:T(1024)(128)(4,1)}), s8[4194304]{0:T(1024)(128)(4,1)S(1)}, s32[]{:S(2)}) async-start(s8[16777216]{0:T(1024)(128)(4,1)} %bitcast.240), calls=%async_computation.7 | async-start | bytes 8388608 | tf_op jit(solution)/shard_map/while
  813.6 237.7 %copy-start.58 = (f32[1024]{0:T(1024)S(1)}, f32[1024]{0:T(1024)}, u32[]{:S(2)}) copy-start(f32[1024]{0:T(1024)} %get-tuple-element.622) | copy-start | bytes 12292
  813.6 237.7 %copy-start.59 = (f32[1024]{0:T(1024)S(1)}, f32[1024]{0:T(1024)}, u32[]{:S(2)}) copy-start(f32[1024]{0:T(1024)} %get-tuple-element.623) | copy-start | bytes 12292
  813.7 237.7 %copy-start.63 = (f32[1024]{0:T(1024)S(1)}, f32[1024]{0:T(1024)}, u32[]{:S(2)}) copy-start(f32[1024]{0:T(1024)} %get-tuple-element.278) | copy-start | bytes 12292
  813.7 237.7 %copy-start.64 = (f32[1024]{0:T(1024)S(1)}, f32[1024]{0:T(1024)}, u32[]{:S(2)}) copy-start(f32[1024]{0:T(1024)} %get-tuple-element.279) | copy-start | bytes 12292
  813.7 237.7 %copy-start.65 = (f32[1024]{0:T(1024)S(1)}, f32[1024]{0:T(1024)}, u32[]{:S(2)}) copy-start(f32[1024]{0:T(1024)} %get-tuple-element.274) | copy-start | bytes 12292
  813.7 237.7 %copy-start.66 = (f32[1024]{0:T(1024)S(1)}, f32[1024]{0:T(1024)}, u32[]{:S(2)}) copy-start(f32[1024]{0:T(1024)} %get-tuple-element.275) | copy-start | bytes 12292
  813.7 237.8 %copy-start.53 = (f32[4096]{0:T(1024)S(1)}, f32[4096]{0:T(1024)}, u32[]{:S(2)}) copy-start(f32[4096]{0:T(1024)} %copy-done.52) | copy-start | bytes 49156
  817.5 278.9 %copy-start.18 = (f32[256,1024]{1,0:T(8,128)}, f32[256,1024]{1,0:T(8,128)S(1)}, u32[]{:S(2)}) copy-start(f32[256,1024]{1,0:T(8,128)S(1)} %convolution_add_fusion) | copy-start | bytes 3145732
  817.5 277.6 %copy-start.70 = (f32[1024]{0:T(1024)S(1)}, f32[1024]{0:T(1024)}, u32[]{:S(2)}) copy-start(f32[1024]{0:T(1024)} %param.35) | copy-start | bytes 12292
  817.6 277.6 %copy-start.71 = (f32[1024]{0:T(1024)S(1)}, f32[1024]{0:T(1024)}, u32[]{:S(2)}) copy-start(f32[1024]{0:T(1024)} %param.51) | copy-start | bytes 12292
  817.6 278.2 %copy-start.47 = (f32[6,1024]{1,0:T(8,128)S(1)}, f32[6,1024]{1,0:T(8,128)}, u32[]{:S(2)}) copy-start(f32[6,1024]{1,0:T(8,128)} %param.37) | copy-start | bytes 73732
  817.6 278.2 %copy-start.56 = (f32[6,1024]{1,0:T(8,128)S(1)}, f32[6,1024]{1,0:T(8,128)}, u32[]{:S(2)}) copy-start(f32[6,1024]{1,0:T(8,128)} %param.53) | copy-start | bytes 73732
  1106.4 215.1 %reduce-scatter.2.cloned.1.call-start = ((), (), s32[]{:S(2)}) async-start(), calls=%async_computation.4 | async-start | bytes 5242880 | tf_op jit(solution)/shard_map/reduce_scatter | solution.py:238
  (75 other events, 633.5 us)
Sparse Core Ops, SparseCore 0:
  106.4 153.2 all-reduce.7
  305.0 153.0 all-reduce.9
  495.8 153.0 all-reduce.11
  1106.5 67.8 all-reduce.13
  1176.8 43.4 reduce-scatter.1
